TPU v7x, 512 devices: a whole 4x4x16 slice. The times are simulated.
512 devices in a mesh: ctx: 64 (over z_hi, x, y, core), pair: 8 (over z_lo).
Axes of the slice: x: 4, y: 4, z: 16 (z_hi: 2, z_lo: 8; z = z_hi * 8 + z_lo), core: 2. Of those that a mesh axis runs over, the one named last changes fastest.
Arguments:
- tokens: bfloat16 [8, 8192, 1536], P('pair', 'ctx'), may hold values from -24 to 24
- w_query: bfloat16 [1536, 512], P('pair'), may hold values from -0.15625 to 0.15625
- w_key: bfloat16 [1536, 128], P('pair'), may hold values from -0.15625 to 0.15625
- w_value: bfloat16 [1536, 192], P('pair'), may hold values from -0.15625 to 0.15625
- w_out: bfloat16 [768, 1536], P('pair'), may hold values from -0.21875 to 0.21875
- norm_gain: float32 [1536], replicated, may hold values from 0.5 to 1.5
- w_pair: bfloat16 [1536, 256], replicated, may hold values from -0.15625 to 0.15625
- conv_weight: bfloat16 [9, 128, 128], replicated, may hold values from -0.1875 to 0.1875
Outputs:
- seq_out: bfloat16 [8, 8192, 1536], P('pair', 'ctx')
- pair_out: bfloat16 [8, 512, 512, 128], P(None, 'ctx', 'pair')
All inputs are finite; a program needn't handle non-finite values.
Results may differ from a plain program's by a relative error of at most 0.014.
The roundings to bfloat16 on the way count: a program that leaves them out, or rounds other values in their place, can miss the bound.
Values may be sent and summed in bfloat16 or wider, within the bound.
A program may use at most 128 MiB of HBM per device.

v0:
```python
import jax
import jax.numpy as jnp
from jax import lax
from jax.sharding import PartitionSpec as P

H = 4
KEY = 128
VAL = 192
PC = 128
POOL = 16
DILATION_STEP = 2


def with_halo(cells, sides, width):
    for axis, dim in sides:
        count = lax.axis_size(axis)
        ends = count - 1
        head = lax.slice_in_dim(cells, 0, width, axis=dim)
        tail = lax.slice_in_dim(cells, cells.shape[dim] - width, cells.shape[dim], axis=dim)
        cells = jnp.concatenate(
            [
                lax.ppermute(tail, axis, [(i, (i + 1) % count) for i in range(ends)]),
                cells,
                lax.ppermute(head, axis, [((i + 1) % count, i) for i in range(ends)]),
            ],
            axis=dim,
        )
    return cells


def on_device(tokens, w_query, w_key, w_value, w_out, norm_gain, w_pair, conv_weight):
    seq_block, row_count, width = tokens.shape
    flat = tokens.reshape(seq_block * row_count, width)
    pieces = (
        lax.all_gather(w_query, "pair", axis=0, tiled=True),
        lax.all_gather(w_key, "pair", axis=0, tiled=True),
        lax.all_gather(w_value, "pair", axis=0, tiled=True),
    )
    columns = flat
    queries, keys, values = tuple(
        (jnp.dot(columns, piece_item, preferred_element_type=jnp.float32) for piece_item in pieces)
    )
    queries = queries.astype(jnp.bfloat16).reshape(seq_block, row_count, H, KEY)
    keys = keys.astype(jnp.bfloat16).reshape(seq_block, row_count, KEY)
    values = values.astype(jnp.bfloat16).reshape(seq_block, row_count, VAL)
    scaling = KEY ** (-0.5)
    highest = jnp.full((seq_block, H, row_count), -1e30, jnp.float32)
    key_piece = lax.all_gather(keys, "ctx", axis=1, tiled=True)
    value_piece = lax.all_gather(values, "ctx", axis=1, tiled=True)
    scores = (
        jnp.einsum("bqhk,bnk->bhqn", queries, key_piece, preferred_element_type=jnp.float32)
        * scaling
    )
    new_high = jnp.maximum(highest, jnp.max(scores, axis=-1))
    weights = jnp.exp(scores - new_high[..., None])
    totals = jnp.sum(weights, axis=-1)
    accum = jnp.einsum(
        "bhqn,bnv->bhqv",
        weights.astype(jnp.bfloat16),
        value_piece,
        preferred_element_type=jnp.float32,
    )
    running = (new_high, totals, accum)
    highest, totals, accum = running
    mixed = (accum / totals[..., None]).astype(jnp.bfloat16)
    mixed = jnp.transpose(mixed, (0, 2, 1, 3)).reshape(seq_block * row_count, H * VAL)
    columns = mixed
    projected = jnp.dot(
        columns,
        lax.all_gather(w_out, "pair", axis=0, tiled=True),
        preferred_element_type=jnp.float32,
    )
    summed = tokens.astype(jnp.float32) + projected.reshape(seq_block, row_count, width)
    seq_out = summed.astype(jnp.bfloat16)
    pooled = jnp.mean(summed.reshape(seq_block, row_count // POOL, POOL, width), axis=2)
    normed = (
        pooled * lax.rsqrt(jnp.mean(pooled * pooled, axis=-1, keepdims=True) + 1e-06) * norm_gain
    )
    normed = normed.astype(jnp.bfloat16)
    averaged_rows = row_count // POOL
    both = jnp.dot(
        normed.reshape(seq_block * averaged_rows, width), w_pair, preferred_element_type=jnp.float32
    ).astype(jnp.bfloat16)
    both = both.reshape(seq_block, averaged_rows, 2 * PC)
    rowpart = both[:, :, :PC]
    colpart = both[:, :, PC:]
    rows_all = lax.all_gather(rowpart, "pair", axis=0, tiled=True)
    ctx_count = lax.axis_size("ctx")
    pair_count = lax.axis_size("pair")
    map_len = averaged_rows * ctx_count
    column_total = map_len // pair_count
    gathered = lax.all_gather(colpart, ("ctx", "pair"), axis=1, tiled=True)
    gathered = gathered.reshape(seq_block, ctx_count, pair_count, averaged_rows, PC)
    gathered = jnp.transpose(gathered, (2, 0, 1, 3, 4)).reshape(pair_count * seq_block, map_len, PC)
    cols_all = lax.dynamic_slice_in_dim(
        gathered, lax.axis_index("pair") * column_total, column_total, 1
    )
    pairwise_grid = (
        rows_all.astype(jnp.float32)[:, :, None, :] * cols_all.astype(jnp.float32)[:, None, :, :]
    ).astype(jnp.bfloat16)
    padded_map = with_halo(pairwise_grid, (("ctx", 1), ("pair", 2)), DILATION_STEP)
    seq_total = pairwise_grid.shape[0]
    cells = seq_total * averaged_rows * column_total
    total = jnp.zeros((cells, PC), jnp.float32)
    for row_offset in range(3):
        for column_offset in range(3):
            kernel_window = padded_map[
                :,
                row_offset * DILATION_STEP : row_offset * DILATION_STEP + averaged_rows,
                column_offset * DILATION_STEP : column_offset * DILATION_STEP + column_total,
                :,
            ]
            total = total + jnp.dot(
                kernel_window.reshape(cells, PC),
                conv_weight[row_offset * 3 + column_offset],
                preferred_element_type=jnp.float32,
            )
    result = pairwise_grid.astype(jnp.float32) + jax.nn.gelu(
        total.reshape(seq_total, averaged_rows, column_total, PC)
    )
    return (seq_out, result.astype(jnp.bfloat16))


def solution(mesh):
    return jax.shard_map(
        on_device,
        mesh=mesh,
        in_specs=(
            P("pair", "ctx", None),
            P("pair", None),
            P("pair", None),
            P("pair", None),
            P("pair", None),
            P(),
            P(),
            P(),
        ),
        out_specs=(P("pair", "ctx", None), P(None, "ctx", "pair", None)),
        check_vma=False,
    )
```

profile of v0, /device:TPU:31, one launch (start us, length us, event | category | flops | bytes accessed | tf_op | source)
XLA Modules:
  0.0 1519.2 jit_solution(11475428438196550576)
XLA Ops:
  7.2 0.7 all-gather.8.cloned.1.call-update
  8.0 46.8 %all_gather.24 = bf16[1536,128]{1,0:T(8,128)(2,1)S(1)} all-gather(bf16[192,128]{1,0:T(8,128)(2,1)} %param.10), channel_id=1, replica_groups=mesh['ctx'=64,'pair'=8] {'pair'}, dimensions={0}, use_global_device_ids=true | all-gather | bytes 442368 | tf_op jit(solution)/shard_map/all_gather | solution.py:36
  54.8 1.9 convolution_convert_fusion.2
  56.8 45.8 %all_gather.27 = bf16[1536,192]{1,0:T(8,128)(2,1)S(1)} all-gather(bf16[192,192]{1,0:T(8,128)(2,1)} %param.11), channel_id=1, replica_groups=mesh['ctx'=64,'pair'=8] {'pair'}, dimensions={0}, use_global_device_ids=true | all-gather | bytes 663552 | tf_op jit(solution)/shard_map/all_gather | solution.py:37
  102.5 1.0 convolution_convert_fusion.1
  103.7 0.5 all-gather.10.cloned.1.call-update
  104.3 1.8 fusion.22
  106.1 90.0 %all-gather.14.cloned.1.call-done = bf16[8192,128]{1,0:T(8,128)(2,1)} async-done(((bf16[128,128]{1,0:T(8,128)(2,1)}), bf16[8192,128]{1,0:T(8,128)(2,1)}) %all-gather.14.cloned.1.call-update) | async-done | bytes 2097168 | tf_op jit(solution)/shard_map/all_gather | solution.py:48
  196.1 9.7 bitcast_reduce_fusion
  205.7 8.5 fusion.1
  214.3 109.7 %all-gather.16.cloned.1.call-done = bf16[8192,192]{0,1:T(8,128)(2,1)} async-done(((bf16[128,192]{0,1:T(8,128)(2,1)}), bf16[8192,192]{0,1:T(8,128)(2,1)}) %all-gather.16.cloned.1.call-update) | async-done | bytes 3145744 | tf_op jit(solution)/shard_map/all_gather | solution.py:49
  324.0 9.7 fusion.29
  333.7 50.9 %all-gather.10.cloned.1.call-done = bf16[768,1536]{1,0:T(8,128)(2,1)} async-done(((bf16[96,1536]{1,0:T(8,128)(2,1)}), bf16[768,1536]{1,0:T(8,128)(2,1)}) %all-gather.10.cloned.1.call-update) | async-done | bytes 2359312 | tf_op jit(solution)/shard_map/all_gather | solution.py:70
  384.6 2.9 fusion.66
  388.1 0.6 fusion.65
  388.7 37.2 %all_gather.30 = bf16[8,8,128]{2,1,0:T(8,128)(2,1)S(1)} all-gather(bf16[1,8,128]{2,1,0:T(8,128)(2,1)S(1)} %get-tuple-element.16), channel_id=1, replica_groups=mesh['ctx'=64,'pair'=8] {'pair'}, dimensions={0}, use_global_device_ids=true | all-gather | bytes 18432 | tf_op jit(solution)/shard_map/all_gather | solution.py:87
  425.9 1024.5 %all-gather.12.cloned.1.call-done = bf16[1,4096,128]{2,1,0:T(8,128)(2,1)} async-done(((bf16[1,8,128]{2,1,0:T(8,128)(2,1)}), bf16[1,4096,128]{2,1,0:T(8,128)(2,1)}) %all-gather.12.cloned.1.call-update) | async-done | bytes 1048592 | tf_op jit(solution)/shard_map/all_gather | solution.py:92
  1450.5 1.4 copy.30
  1452.3 16.6 %collective-permute-start = (bf16[8,2,64,128]{3,2,1,0:T(8,128)(2,1)S(1)}, bf16[8,2,64,128]{3,2,1,0:T(8,128)(2,1)S(1)}, u32[]{:S(2)}, u32[]{:S(2)}) collective-permute-start(bf16[8,2,64,128]{3,2,1,0:T(8,128)(2,1)S(1)} %get-tuple-element.14), channel_id=1, source_target_pairs={{0,8},{8,16},{16,24},{24,32},{32,40},{40,48},{48,56},{56,64},{64,7... | collective-permute-start | bytes 786440 | tf_op jit(solution)/shard_map/ppermute | solution.py:22
  1468.9 1.9 collective-permute-start.1
  1470.8 1.4 collective-permute-done
  1472.2 17.6 %collective-permute-done.1 = bf16[8,2,64,128]{3,2,1,0:T(8,128)(2,1)S(1)} collective-permute-done((bf16[8,2,64,128]{3,2,1,0:T(8,128)(2,1)S(1)}, bf16[8,2,64,128]{3,2,1,0:T(8,128)(2,1)S(1)}, u32[]{:S(2)}, u32[]{:S(2)}) %collective-permute-start.1) | collective-permute-done | bytes 262176 | tf_op jit(solution)/shard_map/ppermute | solution.py:24
  1489.9 10.3 collective-permute-start.2
  1500.3 1.5 collective-permute-start.3
  1502.3 2.8 collective-permute-done.3
  1505.1 1.0 maximum_maximum_fusion
  1506.0 1.4 fusion.62
  1507.9 0.4 convolution_add_fusion.6
  1508.7 0.4 convolution_add_fusion.4
  1509.6 0.4 convolution_add_fusion.2
  1510.4 0.4 fusion.8
  1510.9 1.8 fusion.19
  (36 shorter events, 3.5 us)
Async XLA Ops:
  7.2 380.7 %copy-start = (bf16[1536,256]{1,0:T(8,128)(2,1)S(1)}, bf16[1536,256]{1,0:T(8,128)(2,1)}, u32[]{:S(2)}) copy-start(bf16[1536,256]{1,0:T(8,128)(2,1)} %param.14) | copy-start | bytes 2359300
  7.2 95.4 %copy-start.2 = (bf16[1,128,1536]{2,1,0:T(8,128)(2,1)S(1)}, bf16[1,128,1536]{2,1,0:T(8,128)(2,1)}, u32[]{:S(2)}) copy-start(bf16[1,128,1536]{2,1,0:T(8,128)(2,1)} %param.8) | copy-start | bytes 1179652
  7.2 97.1 %all-gather.8.cloned.1.call-start = ((), (), s32[]{:S(2)}) async-start(), calls=%async_computation | async-start | bytes 1769472 | tf_op jit(solution)/shard_map/all_gather | solution.py:35
  7.9 188.1 %all-gather.14.cloned.1.call-start = ((), (), s32[]{:S(2)}) async-start(), calls=%async_computation.3 | async-start | bytes 2129920 | tf_op jit(solution)/shard_map/all_gather | solution.py:48
  56.7 267.3 %all-gather.16.cloned.1.call-start = ((), (), s32[]{:S(2)}) async-start(), calls=%async_computation.4 | async-start | bytes 3194880 | tf_op jit(solution)/shard_map/all_gather | solution.py:49
  103.6 281.0 %all-gather.10.cloned.1.call-start = ((), (), s32[]{:S(2)}) async-start(), calls=%async_computation.1 | async-start | bytes 2654208 | tf_op jit(solution)/shard_map/all_gather | solution.py:70
  104.2 1346.3 %all-gather.12.cloned.1.call-start = ((), (), s32[]{:S(2)}) async-start(), calls=%async_computation.2 | async-start | bytes 1050624 | tf_op jit(solution)/shard_map/all_gather | solution.py:92
  384.6 3.2 copy-start.4
  1452.3 19.9 %collective-permute-start = (bf16[8,2,64,128]{3,2,1,0:T(8,128)(2,1)S(1)}, bf16[8,2,64,128]{3,2,1,0:T(8,128)(2,1)S(1)}, u32[]{:S(2)}, u32[]{:S(2)}) collective-permute-start(bf16[8,2,64,128]{3,2,1,0:T(8,128)(2,1)S(1)} %get-tuple-element.14), channel_id=1, source_target_pairs={{0,8},{8,16},{16,24},{24,32},{32,40},{40,48},{48,56},{56,64},{64,7... | collective-permute-start | bytes 786440 | tf_op jit(solution)/shard_map/ppermute | solution.py:22
  1468.9 20.9 %collective-permute-start.1 = (bf16[8,2,64,128]{3,2,1,0:T(8,128)(2,1)S(1)}, bf16[8,2,64,128]{3,2,1,0:T(8,128)(2,1)S(1)}, u32[]{:S(2)}, u32[]{:S(2)}) collective-permute-start(bf16[8,2,64,128]{3,2,1,0:T(8,128)(2,1)S(1)} %get-tuple-element.15), channel_id=1, source_target_pairs={{8,0},{16,8},{24,16},{32,24},{40,32},{48,40},{56,48},{64,56},{72,6... | collective-permute-start | bytes 786440 | tf_op jit(solution)/shard_map/ppermute | solution.py:24
  1489.9 12.0 copy-start.3
  1489.9 12.4 collective-permute-start.2
  1500.3 4.8 collective-permute-start.3
  1510.4 2.3 copy-start.1
Sparse Core Ops, SparseCore 0:
  10.1 69.5 all-gather.7
  84.7 111.3 all-gather.13
  200.9 123.1 all-gather.15
  325.9 58.6 all-gather.9
  388.8 1061.5 all-gather.11
where the time goes:
time: 1520 us
  waiting for transfers between devices  1300 us (86%)
  blocking collectives  130 us (9%)
  matrix products  31 us (2%)
  starting transfers between devices  30.5 us (2%)
    all_gather x1, waiting for transfers between devices, on_device(): gathered = lax.all_gather(colpart, ('ctx', 'pair'), axis=1, tiled=True)  1020 us
    all_gather x1, waiting for transfers between devices, on_device(): value_piece = lax.all_gather(values, 'ctx', axis=1, tiled=True)  110 us
    all_gather x1, waiting for transfers between devices, on_device(): key_piece = lax.all_gather(keys, 'ctx', axis=1, tiled=True)  90 us
    all_gather x1, waiting for transfers between devices, on_device(): lax.all_gather(w_out, 'pair', axis=0, tiled=True)  50.9 us
    all_gather x1, blocking collectives, on_device(): lax.all_gather(w_key, 'pair', axis=0, tiled=True)  46.8 us
    all_gather x1, blocking collectives, on_device(): lax.all_gather(w_value, 'pair', axis=0, tiled=True)  45.8 us
    all_gather x1, blocking collectives, on_device(): rows_all = lax.all_gather(rowpart, 'pair', axis=0, tiled=True)  37.2 us
  transfers between devices with their start and end apart: 9, of which 7 were waited for; matrix products, arithmetic and copies ran while one was open for 2% of the time, Pallas kernels for 0%

commit v1 on v0

--- a/solution.py
+++ b/solution.py
@@ -89,7 +89,8 @@
     pair_count = lax.axis_size("pair")
     map_len = averaged_rows * ctx_count
     column_total = map_len // pair_count
-    gathered = lax.all_gather(colpart, ("ctx", "pair"), axis=1, tiled=True)
+    sent = jnp.stack([colpart] * lax.axis_size(("ctx", "pair")))
+    gathered = jnp.concatenate(lax.all_to_all(sent, ("ctx", "pair"), 0, 0), axis=1)
     gathered = gathered.reshape(seq_block, ctx_count, pair_count, averaged_rows, PC)
     gathered = jnp.transpose(gathered, (2, 0, 1, 3, 4)).reshape(pair_count * seq_block, map_len, PC)
     cols_all = lax.dynamic_slice_in_dim(

time: 1520 us -> 543 us (0.36)
  waiting for transfers between devices: 1300 us -> 274 us
  blocking collectives: 130 us -> 164 us
    all_gather x1 -> x0, waiting for transfers between devices: 1020 us -> none  [on_device(): gathered = lax.all_gather(colpart, ('ctx', 'pair'), axis=1, tiled=True)]
    all_gather x1, blocking collectives: 37.2 us -> 71.8 us  [on_device(): rows_all = lax.all_gather(rowpart, 'pair', axis=0, tiled=True)]
    all_to_all x0 -> x1, starting transfers between devices: none -> 19.8 us  [on_device(): lax.all_to_all(sent, ('ctx', 'pair'), 0, 0)]
  transfers between devices with their start and end apart: 9 -> 9, of which waited for: 7 -> 6; matrix products, arithmetic and copies ran while one was open for 2% -> 6% of each run, Pallas kernels for 0% -> 0%
where the time goes in v1:
time: 543 us; the launch traced here: 542 us
  waiting for transfers between devices  274 us (50%)
  blocking collectives  164 us (30%)
  starting transfers between devices  44.4 us (8%)
  matrix products  31 us (6%)
  between operations  14 us (3%)
  other arithmetic  12.1 us (2%)
    all_gather x1, waiting for transfers between devices, on_device(): value_piece = lax.all_gather(values, 'ctx', axis=1, tiled=True)  110 us
    all_gather x1, waiting for transfers between devices, on_device(): key_piece = lax.all_gather(keys, 'ctx', axis=1, tiled=True)  90.1 us
    all_gather x1, blocking collectives, on_device(): rows_all = lax.all_gather(rowpart, 'pair', axis=0, tiled=True)  71.8 us
    all_gather x1, waiting for transfers between devices, on_device(): lax.all_gather(w_out, 'pair', axis=0, tiled=True)  50.9 us
    all_gather x1, blocking collectives, on_device(): lax.all_gather(w_key, 'pair', axis=0, tiled=True)  46.8 us
    all_gather x1, blocking collectives, on_device(): lax.all_gather(w_value, 'pair', axis=0, tiled=True)  45.8 us
    ppermute x2, starting transfers between devices, with_halo(): lax.ppermute(tail, axis, [(i, (i + 1) % count) for i in range(ends)])  21.3 us
    ppermute x2, waiting for transfers between devices, with_halo(): lax.ppermute(head, axis, [((i + 1) % count, i) for i in range(ends)])  20.3 us
  transfers between devices with their start and end apart: 9, of which 6 were waited for; matrix products, arithmetic and copies ran while one was open for 6% of the time, Pallas kernels for 0%

profile of v1, /device:TPU:31, one launch (start us, length us, event | category | flops | bytes accessed | tf_op | source)
XLA Modules:
  0.0 542.4 jit_solution(7918311177929019047)
XLA Ops:
  7.2 0.7 all-gather.7.cloned.1.call-update
  8.0 46.8 %all_gather.21 = bf16[1536,128]{1,0:T(8,128)(2,1)S(1)} all-gather(bf16[192,128]{1,0:T(8,128)(2,1)} %param.10), channel_id=1, replica_groups=mesh['ctx'=64,'pair'=8] {'pair'}, dimensions={0}, use_global_device_ids=true | all-gather | bytes 442368 | tf_op jit(solution)/shard_map/all_gather | solution.py:36
  54.8 1.9 convolution_convert_fusion.2
  56.8 45.8 %all_gather.24 = bf16[1536,192]{1,0:T(8,128)(2,1)S(1)} all-gather(bf16[192,192]{1,0:T(8,128)(2,1)} %param.11), channel_id=1, replica_groups=mesh['ctx'=64,'pair'=8] {'pair'}, dimensions={0}, use_global_device_ids=true | all-gather | bytes 663552 | tf_op jit(solution)/shard_map/all_gather | solution.py:37
  102.5 1.0 convolution_convert_fusion.1
  103.7 0.5 all-gather.9.cloned.1.call-update
  104.2 1.8 fusion.22
  106.0 90.1 %all-gather.11.cloned.1.call-done = bf16[8192,128]{1,0:T(8,128)(2,1)} async-done(((bf16[128,128]{1,0:T(8,128)(2,1)}), bf16[8192,128]{1,0:T(8,128)(2,1)}) %all-gather.11.cloned.1.call-update) | async-done | bytes 2097168 | tf_op jit(solution)/shard_map/all_gather | solution.py:48
  196.1 9.7 %bitcast_reduce_fusion = (f32[4,128]{1,0:T(4,128)S(1)}, f32[8192,128,4]{1,0,2:T(8,128)}) fusion(bf16[16,4,8,128]{3,2,1,0:T(8,128)(2,1)S(1)} %fusion.22, bf16[8192,128]{1,0:T(8,128)(2,1)} %all-gather.11.cloned.1.call-done), kind=kOutput, calls=%fused_computation.1 | convolution fusion | flops 1082129920 | bytes 19007488 | tf_op jit(solution)/shard_map/bqhk,bnk->bhqn/dot_general | solution.py:51
  205.7 8.5 %fusion.1 = f32[4,128]{1,0:T(4,128)S(1)} fusion(f32[8192,128,4]{1,0,2:T(8,128)} %get-tuple-element.19, f32[4,128]{1,0:T(4,128)S(1)} %broadcast_maximum_fusion), kind=kLoop, calls=%fused_computation.3 | loop fusion | flops 12582400 | bytes 16781312 | tf_op jit(solution)/shard_map/reduce_sum | solution.py:56
  214.3 109.7 %all-gather.13.cloned.1.call-done = bf16[8192,192]{0,1:T(8,128)(2,1)} async-done(((bf16[128,192]{0,1:T(8,128)(2,1)}), bf16[8192,192]{0,1:T(8,128)(2,1)}) %all-gather.13.cloned.1.call-update) | async-done | bytes 3145744 | tf_op jit(solution)/shard_map/all_gather | solution.py:49
  324.0 9.7 %fusion.29 = bf16[4,128,192]{1,2,0:T(8,128)(2,1)S(1)} fusion(f32[8192,128,4]{1,0,2:T(8,128)} %get-tuple-element.19, f32[4,128]{1,0:T(4,128)S(1)} %broadcast_maximum_fusion, bf16[8192,192]{0,1:T(8,128)(2,1)} %all-gather.13.cloned.1.call-done, f32[4,128]{1,0:T(4,128)S(1)} %fusion.1), kind=kOutput, calls=%fused_computation.45 | convolution fusion | flops 1623392256 | bytes 20123648 | tf_op jit(solution)/shard_map/bhqn,bnv->bhqv/dot_general | solution.py:57
  333.7 50.9 %all-gather.9.cloned.1.call-done = bf16[768,1536]{1,0:T(8,128)(2,1)} async-done(((bf16[96,1536]{1,0:T(8,128)(2,1)}), bf16[768,1536]{1,0:T(8,128)(2,1)}) %all-gather.9.cloned.1.call-update) | async-done | bytes 2359312 | tf_op jit(solution)/shard_map/all_gather | solution.py:70
  384.6 2.9 fusion.66
  388.1 1.1 stack.2
  389.2 19.8 %all-to-all-start = ((bf16[512,1,8,128]{3,2,1,0:T(8,128)(2,1)}), bf16[512,1,8,128]{3,2,1,0:T(8,128)(2,1)S(1)}, u32[]{:S(2)}, u32[]{:S(2)}) async-start(bf16[512,1,8,128]{3,2,1,0:T(8,128)(2,1)} %stack.2), calls=%async_computation | async-start | bytes 2097152 | tf_op jit(solution)/shard_map/all_to_all | solution.py:93
  409.0 71.8 %all_gather.27 = bf16[8,8,128]{2,1,0:T(8,128)(2,1)S(1)} all-gather(bf16[1,8,128]{2,1,0:T(8,128)(2,1)S(1)} %get-tuple-element.16), channel_id=1, replica_groups=mesh['ctx'=64,'pair'=8] {'pair'}, dimensions={0}, use_global_device_ids=true | all-gather | bytes 18432 | tf_op jit(solution)/shard_map/all_gather | solution.py:87
  481.4 15.9 %collective-permute-start = (bf16[8,2,64,128]{3,2,1,0:T(8,128)(2,1)S(1)}, bf16[8,2,64,128]{3,2,1,0:T(8,128)(2,1)S(1)}, u32[]{:S(2)}, u32[]{:S(2)}) collective-permute-start(bf16[8,2,64,128]{3,2,1,0:T(8,128)(2,1)S(1)} %get-tuple-element.14), channel_id=1, source_target_pairs={{0,8},{8,16},{16,24},{24,32},{32,40},{40,48},{48,56},{56,64},{64,7... | collective-permute-start | bytes 786440 | tf_op jit(solution)/shard_map/ppermute | solution.py:22
  497.3 1.9 collective-permute-start.1
  499.3 1.4 collective-permute-done
  500.6 17.4 %collective-permute-done.1 = bf16[8,2,64,128]{3,2,1,0:T(8,128)(2,1)S(1)} collective-permute-done((bf16[8,2,64,128]{3,2,1,0:T(8,128)(2,1)S(1)}, bf16[8,2,64,128]{3,2,1,0:T(8,128)(2,1)S(1)}, u32[]{:S(2)}, u32[]{:S(2)}) %collective-permute-start.1) | collective-permute-done | bytes 262176 | tf_op jit(solution)/shard_map/ppermute | solution.py:24
  518.1 5.4 collective-permute-start.2
  523.5 1.3 collective-permute-start.3
  525.4 2.9 collective-permute-done.3
  528.3 1.0 maximum_maximum_fusion
  529.3 1.4 fusion.62
  531.5 0.4 convolution_add_fusion.5
  532.4 0.4 convolution_add_fusion.3
  532.8 0.4 convolution_add_fusion.2
  533.2 0.4 convolution_add_fusion.1
  533.7 0.4 fusion.8
  534.1 1.8 fusion.19
  (36 shorter events, 3.2 us)
Async XLA Ops:
  7.2 380.7 %copy-start = (bf16[1536,256]{1,0:T(8,128)(2,1)S(1)}, bf16[1536,256]{1,0:T(8,128)(2,1)}, u32[]{:S(2)}) copy-start(bf16[1536,256]{1,0:T(8,128)(2,1)} %param.14) | copy-start | bytes 2359300
  7.2 95.4 %copy-start.2 = (bf16[1,128,1536]{2,1,0:T(8,128)(2,1)S(1)}, bf16[1,128,1536]{2,1,0:T(8,128)(2,1)}, u32[]{:S(2)}) copy-start(bf16[1,128,1536]{2,1,0:T(8,128)(2,1)} %param.8) | copy-start | bytes 1179652
  7.2 97.0 %all-gather.7.cloned.1.call-start = ((), (), s32[]{:S(2)}) async-start(), calls=%async_computation.1 | async-start | bytes 1769472 | tf_op jit(solution)/shard_map/all_gather | solution.py:35
  7.9 188.1 %all-gather.11.cloned.1.call-start = ((), (), s32[]{:S(2)}) async-start(), calls=%async_computation.3 | async-start | bytes 2129920 | tf_op jit(solution)/shard_map/all_gather | solution.py:48
  56.7 267.3 %all-gather.13.cloned.1.call-start = ((), (), s32[]{:S(2)}) async-start(), calls=%async_computation.4 | async-start | bytes 3194880 | tf_op jit(solution)/shard_map/all_gather | solution.py:49
  103.6 281.0 %all-gather.9.cloned.1.call-start = ((), (), s32[]{:S(2)}) async-start(), calls=%async_computation.2 | async-start | bytes 2654208 | tf_op jit(solution)/shard_map/all_gather | solution.py:70
  384.6 3.2 copy-start.4
  389.2 91.6 %all-to-all-start = ((bf16[512,1,8,128]{3,2,1,0:T(8,128)(2,1)}), bf16[512,1,8,128]{3,2,1,0:T(8,128)(2,1)S(1)}, u32[]{:S(2)}, u32[]{:S(2)}) async-start(bf16[512,1,8,128]{3,2,1,0:T(8,128)(2,1)} %stack.2), calls=%async_computation | async-start | bytes 2097152 | tf_op jit(solution)/shard_map/all_to_all | solution.py:93
  481.4 19.2 %collective-permute-start = (bf16[8,2,64,128]{3,2,1,0:T(8,128)(2,1)S(1)}, bf16[8,2,64,128]{3,2,1,0:T(8,128)(2,1)S(1)}, u32[]{:S(2)}, u32[]{:S(2)}) collective-permute-start(bf16[8,2,64,128]{3,2,1,0:T(8,128)(2,1)S(1)} %get-tuple-element.14), channel_id=1, source_target_pairs={{0,8},{8,16},{16,24},{24,32},{32,40},{40,48},{48,56},{56,64},{64,7... | collective-permute-start | bytes 786440 | tf_op jit(solution)/shard_map/ppermute | solution.py:22
  497.3 20.7 %collective-permute-start.1 = (bf16[8,2,64,128]{3,2,1,0:T(8,128)(2,1)S(1)}, bf16[8,2,64,128]{3,2,1,0:T(8,128)(2,1)S(1)}, u32[]{:S(2)}, u32[]{:S(2)}) collective-permute-start(bf16[8,2,64,128]{3,2,1,0:T(8,128)(2,1)S(1)} %get-tuple-element.15), channel_id=1, source_target_pairs={{8,0},{16,8},{24,16},{32,24},{40,32},{48,40},{56,48},{64,56},{72,6... | collective-permute-start | bytes 786440 | tf_op jit(solution)/shard_map/ppermute | solution.py:24
  518.1 6.9 %copy-start.3 = (bf16[9,128,128]{2,1,0:T(8,128)(2,1)S(1)}, bf16[9,128,128]{2,1,0:T(8,128)(2,1)}, u32[]{:S(2)}) copy-start(bf16[9,128,128]{2,1,0:T(8,128)(2,1)} %param.15) | copy-start | bytes 884740
  518.1 7.3 %collective-permute-start.2 = (bf16[8,12,2,128]{3,2,1,0:T(2,128)(2,1)S(1)}, bf16[8,12,2,128]{3,2,1,0:T(2,128)(2,1)S(1)}, u32[]{:S(2)}, u32[]{:S(2)}) collective-permute-start(bf16[8,12,2,128]{3,2,1,0:T(2,128)(2,1)S(1)} %get-tuple-element.10), channel_id=1, source_target_pairs={{0,1},{1,2},{2,3},{3,4},{4,5},{5,6},{6,7},{8,9},{9,10},{10,11},{11... | collective-permute-start | bytes 147464 | tf_op jit(solution)/shard_map/ppermute | solution.py:22
  523.5 4.8 collective-permute-start.3
  533.6 2.3 copy-start.1
Sparse Core Ops, SparseCore 0:
  10.1 69.5 all-gather.6
  84.7 111.3 all-gather.10
  200.9 123.1 all-gather.12
  325.9 58.6 all-gather.8
